TPU v7x, 32 devices: a whole 2x2x4 slice. The times are simulated.
32 devices in a mesh: group: 4 (over y, x), shard: 8 (over z, core).
Axes of the slice: x: 2, y: 2, z: 4, core: 2. Of those that a mesh axis runs over, the one named last changes fastest.
Arguments:
- tokens: bfloat16 [32, 192, 768], P(('group', 'shard')), may hold values from -650 to 650
- norm_gain: float32 [768], replicated, may hold values from 0.1 to 1.9
- w_query: bfloat16 [768, 768], P('shard'), may hold values from -8 to 8
- w_key: bfloat16 [768, 768], P('shard'), may hold values from -0.21875 to 0.21875
- w_value: bfloat16 [768, 768], P('shard'), may hold values from -0.625 to 0.625
- w_out: bfloat16 [768, 768], P('shard'), may hold values from -0.21875 to 0.21875
- owner_map: int32 [4, 8], P('group'), may hold values from 0 to 7, each once within a row
- pair_images: int32 [256, 2], P(('group', 'shard')), may hold values from 0 to 7, as said below
- pair_count: int32 [32], P(('group', 'shard')), may hold values from 1 to 8, 128 in all
- confidence: int32 [256, 2], P(('group', 'shard')), may hold values from 1 to 8
Outputs:
- updated: bfloat16 [32, 192, 768], P(('group', 'shard'))
Inputs may be any that keep to these rules, and one draw needn't show every extreme that they name: `pair_images`: each row names two different images of the listing device's own group, by their index within that group. Device d lists its pairs in its first pair_count[d] rows of pair_images and confidence; the other rows are unused.
All inputs are finite; a program needn't handle non-finite values.
Results may differ from a plain program's by a relative error of at most 0.013.
The roundings to bfloat16 on the way count: a program that leaves them out, or rounds other values in their place, can miss the bound.
Values may be sent and summed in bfloat16 or wider, within the bound.
No kernel may reach another device: no remote copies, remote signals or barrier semaphores. Data moves between devices by JAX's collectives and lax.ppermute only.
A program may use at most 128 MiB of HBM per device.

v0:
```python
import math
import jax
import jax.numpy as jnp
from jax import lax
from jax.sharding import PartitionSpec as P

HEADS = 12
HEAD_DIM = 64


def layer_norm(values, norm_gain):
    values = values.astype(jnp.float32)
    average = jnp.mean(values, axis=-1, keepdims=True)
    centred = values - average
    variance = jnp.mean(centred * centred, axis=-1, keepdims=True)
    return (centred * lax.rsqrt(variance + 1e-05) * norm_gain).astype(jnp.bfloat16)


def attend_many(queries, keys_many, values_many, out_weight):
    count = queries.shape[0]
    length = queries.shape[1]
    query_heads = queries.reshape(count, length, HEADS, HEAD_DIM)
    key_heads = keys_many.reshape(count, length, HEADS, HEAD_DIM)
    value_heads = values_many.reshape(count, length, HEADS, HEAD_DIM)
    scores = jnp.einsum(
        "bqhd,bkhd->bhqk", query_heads, key_heads, preferred_element_type=jnp.float32
    )
    scores = scores * (1.0 / math.sqrt(HEAD_DIM))
    scores = scores - jnp.max(scores, axis=-1, keepdims=True)
    expo = jnp.exp(scores)
    attention = (expo / jnp.sum(expo, axis=-1, keepdims=True)).astype(jnp.bfloat16)
    attended = jnp.einsum(
        "bhqk,bkhd->bqhd", attention, value_heads, preferred_element_type=jnp.float32
    )
    attended = attended.reshape(count * length, HEADS * HEAD_DIM).astype(jnp.bfloat16)
    projected = jnp.dot(attended, out_weight, preferred_element_type=jnp.float32)
    return projected.reshape(count, length, HEADS * HEAD_DIM)


def project_rows(rows, weight):
    return jnp.dot(rows, weight, preferred_element_type=jnp.float32).astype(jnp.bfloat16)


def shards(
    tokens,
    norm_gain,
    w_query,
    w_key,
    w_value,
    w_out,
    owner_map,
    pair_images,
    pair_count,
    confidence,
):
    normed = layer_norm(tokens[0], norm_gain)
    query_weight, key_weight, value_weight, out_weight = (
        lax.all_gather(w_query, "shard", axis=0, tiled=True),
        lax.all_gather(w_key, "shard", axis=0, tiled=True),
        lax.all_gather(w_value, "shard", axis=0, tiled=True),
        lax.all_gather(w_out, "shard", axis=0, tiled=True),
    )
    owners = owner_map[0]
    position = lax.axis_index("shard")
    length = normed.shape[0]
    width = normed.shape[1]
    every_image = lax.all_gather(normed[None], "shard", axis=0, tiled=True)

    def fetch_pair(stored):
        picture = every_image[stored]
        return (project_rows(picture, key_weight), project_rows(picture, value_weight))

    group_pairs, group_conf, group_counts = (
        lax.all_gather(pair_images, "shard", axis=0, tiled=True),
        lax.all_gather(confidence, "shard", axis=0, tiled=True),
        lax.all_gather(pair_count, "shard", axis=0, tiled=True),
    )
    capacity = pair_images.shape[0]
    slot_total = group_pairs.shape[0]
    slot_ids = jnp.arange(slot_total, dtype=jnp.int32)
    usable = slot_ids % capacity < group_counts[slot_ids // capacity]
    store_first = owners[group_pairs[:, 0]]
    store_second = owners[group_pairs[:, 1]]
    querying = jnp.concatenate([store_first, store_second])
    attended_store = jnp.concatenate([store_second, store_first])
    weights_all = jnp.concatenate([group_conf[:, 0], group_conf[:, 1]])
    valid = jnp.concatenate([usable, usable]) & (querying == position)
    direction_ids = jnp.arange(2 * slot_total, dtype=jnp.int32)
    sort_key = jnp.where(valid, direction_ids, 2 * slot_total)
    ordering = jnp.argsort(sort_key)
    chosen_target = attended_store[ordering]
    chosen_weight = weights_all[ordering]
    direction_total = jnp.sum(valid.astype(jnp.int32))
    own_query_rows = project_rows(normed, query_weight)

    def one_direction(number, carried):
        numerator, weight_total = carried
        target_key, target_value = fetch_pair(chosen_target[number])
        projected = attend_many(
            own_query_rows[None], target_key[None], target_value[None], out_weight
        )[0]
        weight_now = chosen_weight[number].astype(jnp.float32)
        return (numerator + weight_now * projected, weight_total + weight_now)

    start = (jnp.zeros((length, width), jnp.float32), jnp.zeros((), jnp.float32))
    numerator, weight_total = lax.fori_loop(0, direction_total, one_direction, start)
    return (numerator / (1.0 + weight_total))[None].astype(jnp.bfloat16)


def solution(mesh):
    in_specs = (
        P(("group", "shard"), None, None),
        P(),
        P("shard", None),
        P("shard", None),
        P("shard", None),
        P("shard", None),
        P("group", None),
        P(("group", "shard"), None),
        P(("group", "shard")),
        P(("group", "shard"), None),
    )
    out_specs = P(("group", "shard"), None, None)
    return jax.shard_map(shards, mesh=mesh, in_specs=in_specs, out_specs=out_specs, check_vma=False)
```

profile of v0, /device:TPU:13, one launch (start us, length us, event | category | flops | bytes accessed | tf_op | source)
XLA Modules:
  0.0 329.1 jit_solution(8869138718722402393)
XLA Ops:
  14.7 6.6 %all-reduce = s32[8]{0:T(128)S(1)} all-reduce(s32[8]{0:T(128)S(1)} %dynamic-update-slice), channel_id=1, replica_groups=mesh['group'=4,'shard'=8] {'shard'}, use_global_device_ids=true, to_apply=%add | all-reduce | flops 8 | bytes 64
  21.3 12.0 %all-gather = s32[8,8,2]{1,2,0:T(2,128)S(1)} all-gather(s32[1,8,2]{1,2,0:T(2,128)S(1)} %bitcast.138), channel_id=1, replica_groups=mesh['group'=4,'shard'=8] {'shard'}, dimensions={0}, use_global_device_ids=true | all-gather | bytes 576 | tf_op jit(solution)/shard_map/all_gather | solution.py:74
  33.4 9.4 %all-gather.1 = s32[8,8,2]{1,2,0:T(2,128)S(1)} all-gather(s32[1,8,2]{1,2,0:T(2,128)S(1)} %bitcast.139), channel_id=1, replica_groups=mesh['group'=4,'shard'=8] {'shard'}, dimensions={0}, use_global_device_ids=true | all-gather | bytes 576 | tf_op jit(solution)/shard_map/all_gather | solution.py:75
  43.6 5.0 %fusion.31 = pred[64]{0:T(512)(128)(4,1)S(1)} fusion(s32[]{:T(128)} %bitcast.13, s32[]{:T(128)} %bitcast.14, s32[]{:T(128)} %bitcast.15, s32[]{:T(128)} %bitcast.16, s32[]{:T(128)} %bitcast.17, s32[]{:T(128)} %bitcast.19, s32[]{:T(128)} %bitcast.18, s32[]{:T(128)} %bitcast.12), kind=kLoop, calls=%fused_computation.74 | loop fusion | flops 2048 | bytes 96 | tf_op jit(solution)/shard_map/lt | solution.py:81
  49.3 5.0 %bitcast_select_fusion.1 = (s32[64]{0:T(128)S(1)}, s32[64]{0:T(128)S(1)}) fusion(s32[64,2]{0,1:T(2,128)S(1)} %reshape.279, s32[]{:T(128)} %bitcast.24, s32[]{:T(128)} %bitcast.25, s32[]{:T(128)} %bitcast.26, s32[]{:T(128)} %bitcast.27, s32[]{:T(128)} %bitcast.28, s32[]{:T(128)} %bitcast.30, s32[]{:T(128)} %bitcast.29, s32[]{:T(128)} %bitcast.23), kind=kLoop, calls=%fused_computation.48 | loop fusion | flops 2176 | bytes 1056 | tf_op jit(solution)/shard_map/gather | solution.py:82
  54.4 2.6 sort.17
  60.2 1.7 convolution_convert_fusion.3
  62.1 19.3 %all-gather.10.cloned.1.call-done = bf16[768,768]{1,0:T(8,128)(2,1)} async-done(((bf16[96,768]{1,0:T(8,128)(2,1)}), bf16[768,768]{1,0:T(8,128)(2,1)}) %all-gather.10.cloned.1.call-update) | async-done | bytes 1179664 | tf_op jit(solution)/shard_map/all_gather | solution.py:60
  81.5 24.0 %all-gather.16.cloned.1.call-done = bf16[768,768]{1,0:T(8,128)(2,1)} async-done(((bf16[96,768]{1,0:T(8,128)(2,1)}), bf16[768,768]{1,0:T(8,128)(2,1)}) %all-gather.16.cloned.1.call-update) | async-done | bytes 1179664 | tf_op jit(solution)/shard_map/all_gather | solution.py:61
  105.4 32.5 %all-gather.8.cloned.1.call-done = bf16[8,192,768]{2,1,0:T(8,128)(2,1)} async-done(((bf16[1,192,768]{2,1,0:T(8,128)(2,1)}), bf16[8,192,768]{2,1,0:T(8,128)(2,1)}) %all-gather.8.cloned.1.call-update) | async-done | bytes 2359312 | tf_op jit(solution)/shard_map/all_gather | solution.py:67
  138.0 183.8 %while.12 = (s32[]{:T(128)}, f32[192,768]{1,0:T(8,128)S(1)}, f32[]{:T(128)}, s32[]{:T(128)}, s32[128]{0:T(128)S(1)}, /*index=5*/s32[128]{0:T(128)S(1)}, bf16[8,1...) while((s32[]{:T(128)}, f32[192,768]{1,0:T(8,128)S(1)}, ...), condition=%wide.region_7.8_spmd, body=%wide.region_4.7_spmd.sunk | while | flops 795672768 | bytes 21547336 | solution.py:106
  142.4 1.9 convolution_convert_fusion.8
  146.0 2.4 fusion.68
  148.4 2.1 convolution_convert_fusion.9
  155.5 1.9 convolution_convert_fusion.8
  157.5 1.4 convolution_convert_fusion.7
  159.1 2.4 fusion.68
  161.5 2.1 convolution_convert_fusion.9
  168.6 1.9 convolution_convert_fusion.8
  170.6 1.4 convolution_convert_fusion.7
  172.2 2.4 fusion.68
  174.6 2.1 convolution_convert_fusion.9
  181.7 1.9 convolution_convert_fusion.8
  183.7 1.4 convolution_convert_fusion.7
  185.3 2.4 fusion.68
  187.7 2.1 convolution_convert_fusion.9
  194.7 1.9 convolution_convert_fusion.8
  196.8 1.4 convolution_convert_fusion.7
  198.4 2.4 fusion.68
  200.7 2.1 convolution_convert_fusion.9
  207.8 1.9 convolution_convert_fusion.8
  209.9 1.4 convolution_convert_fusion.7
  211.4 2.4 fusion.68
  213.8 2.1 convolution_convert_fusion.9
  220.9 1.9 convolution_convert_fusion.8
  223.0 1.4 convolution_convert_fusion.7
  224.5 2.4 fusion.68
  226.9 2.1 convolution_convert_fusion.9
  234.0 1.9 convolution_convert_fusion.8
  236.1 1.4 convolution_convert_fusion.7
  237.6 2.4 fusion.68
  240.0 2.1 convolution_convert_fusion.9
  247.1 1.9 convolution_convert_fusion.8
  249.1 1.4 convolution_convert_fusion.7
  250.7 2.4 fusion.68
  253.1 2.1 convolution_convert_fusion.9
  260.2 1.9 convolution_convert_fusion.8
  262.2 1.4 convolution_convert_fusion.7
  263.8 2.4 fusion.68
  266.2 2.1 convolution_convert_fusion.9
  273.3 1.9 convolution_convert_fusion.8
  275.3 1.4 convolution_convert_fusion.7
  276.9 2.4 fusion.68
  279.3 2.1 convolution_convert_fusion.9
  286.3 1.9 convolution_convert_fusion.8
  288.4 1.4 convolution_convert_fusion.7
  290.0 2.4 fusion.68
  292.3 2.1 convolution_convert_fusion.9
  299.4 1.9 convolution_convert_fusion.8
  303.0 2.4 fusion.68
  305.4 2.1 convolution_convert_fusion.9
  312.5 1.9 convolution_convert_fusion.8
  316.1 2.4 fusion.68
  318.5 2.1 convolution_convert_fusion.9
  (179 shorter events, 45.8 us)
Async XLA Ops:
  6.5 6.8 %copy-start.7 = (u32[32]{0:T(128)S(1)}, u32[32]{0:T(128)}, u32[]{:S(2)}) copy-start(u32[32]{0:T(128)} %constant.98) | copy-start | bytes 388
  6.5 5.2 %copy-start.2 = (bf16[1,192,768]{2,1,0:T(8,128)(2,1)S(1)}, bf16[1,192,768]{2,1,0:T(8,128)(2,1)}, u32[]{:S(2)}) copy-start(bf16[1,192,768]{2,1,0:T(8,128)(2,1)} %param.12) | copy-start | bytes 884740
  6.5 5.2 %copy-start.4 = (f32[768]{0:T(1024)S(1)}, f32[768]{0:T(1024)}, u32[]{:S(2)}) copy-start(f32[768]{0:T(1024)} %param.13) | copy-start | bytes 9220
  6.5 14.8 %copy-start.5 = (s32[8,2]{0,1:T(2,128)S(1)}, s32[8,2]{0,1:T(2,128)}, u32[]{:S(2)}) copy-start(s32[8,2]{0,1:T(2,128)} %param.19) | copy-start | bytes 196
  6.5 26.9 %copy-start.6 = (s32[8,2]{0,1:T(2,128)S(1)}, s32[8,2]{0,1:T(2,128)}, u32[]{:S(2)}) copy-start(s32[8,2]{0,1:T(2,128)} %param.21) | copy-start | bytes 196
  6.5 42.0 %copy-start.3 = (s32[1,8]{1,0:T(1,128)S(1)}, s32[1,8]{1,0:T(1,128)}, u32[]{:S(2)}) copy-start(s32[1,8]{1,0:T(1,128)} %param.18) | copy-start | bytes 100
  6.6 53.7 %all-gather.14.cloned.1.call-start = ((), (), s32[]{:S(2)}) async-start(), calls=%async_computation.3 | async-start | bytes 1327104 | tf_op jit(solution)/shard_map/all_gather | solution.py:58
  7.3 54.8 %all-gather.12.cloned.1.call-start = ((), (), s32[]{:S(2)}) async-start(), calls=%async_computation.2 | async-start | bytes 1327104 | tf_op jit(solution)/shard_map/all_gather | solution.py:59
  8.0 73.4 %all-gather.10.cloned.1.call-start = ((), (), s32[]{:S(2)}) async-start(), calls=%async_computation.1 | async-start | bytes 1327104 | tf_op jit(solution)/shard_map/all_gather | solution.py:60
  8.8 96.6 %all-gather.16.cloned.1.call-start = ((), (), s32[]{:S(2)}) async-start(), calls=%async_computation.4 | async-start | bytes 1327104 | tf_op jit(solution)/shard_map/all_gather | solution.py:61
  9.4 128.6 %all-gather.8.cloned.1.call-start = ((), (), s32[]{:S(2)}) async-start(), calls=%async_computation | async-start | bytes 2654208 | tf_op jit(solution)/shard_map/all_gather | solution.py:67
  142.4 2.1 copy-start
  148.4 2.1 copy-start.1
  155.5 2.1 copy-start
  161.5 2.1 copy-start.1
  168.6 2.1 copy-start
  174.6 2.1 copy-start.1
  181.6 2.1 copy-start
  187.7 2.1 copy-start.1
  194.7 2.1 copy-start
  200.7 2.1 copy-start.1
  207.8 2.1 copy-start
  213.8 2.1 copy-start.1
  220.9 2.1 copy-start
  226.9 2.1 copy-start.1
  234.0 2.1 copy-start
  240.0 2.1 copy-start.1
  247.1 2.1 copy-start
  253.1 2.1 copy-start.1
  260.2 2.1 copy-start
  266.2 2.1 copy-start.1
  273.3 2.1 copy-start
  279.3 2.1 copy-start.1
  286.3 2.1 copy-start
  292.3 2.1 copy-start.1
  299.4 2.1 copy-start
  305.4 2.1 copy-start.1
  312.5 2.1 copy-start
  318.5 2.1 copy-start.1
Sparse Core Ops, SparseCore 0:
  9.0 24.2 all-gather.13
  34.9 22.3 all-gather.11
  59.0 22.4 all-gather.9
  83.0 22.4 all-gather.15
  106.9 30.9 all-gather.7
where the time goes:
time: 331 us; the launch traced here: 329 us
  matrix products  117 us (35%)
  waiting for transfers between devices  78.4 us (24%)
  loops' own time  47 us (14%)
  blocking collectives  28 us (8%)
  local copies, waits for them, and re-layouts  26.9 us (8%)
  other arithmetic  17.4 us (5%)
  between operations  13.9 us (4%)
    dot_general x29, matrix products, project_rows(): jnp.dot(rows, weight, preferred_element_type=jnp.float32)  47 us
    another operation x1, loops' own time, shards(): lax.fori_loop(0, direction_total, one_direction, start)  47 us
    sub x14, matrix products, attend_many(): scores = scores - jnp.max(scores, axis=-1, keepdims=True)  33.4 us
    all_gather x1, waiting for transfers between devices, shards(): every_image = lax.all_gather(normed[None], 'shard', axis=0, tiled=True)  32.5 us
    dot_general x14, matrix products, attend_many(): jnp.einsum('bhqk,bkhd->bqhd', attention, value_heads, preferred_element_t...  29.7 us
    all_gather x1, waiting for transfers between devices, shards(): lax.all_gather(w_out, 'shard', axis=0, tiled=True)  24 us
    all_gather x1, waiting for transfers between devices, shards(): lax.all_gather(w_value, 'shard', axis=0, tiled=True)  19.3 us
    all_gather x1, blocking collectives, shards(): lax.all_gather(pair_images, 'shard', axis=0, tiled=True)  12 us
  transfers between devices with their start and end apart: 5, of which 3 were waited for; matrix products, arithmetic and copies ran while one was open for 7% of the time, Pallas kernels for 0%

commit v1 on v0

--- a/solution.py
+++ b/solution.py
@@ -64,7 +64,14 @@
     position = lax.axis_index("shard")
     length = normed.shape[0]
     width = normed.shape[1]
-    every_image = lax.all_gather(normed[None], "shard", axis=0, tiled=True)
+    ring = [normed[None]]
+    for hop in range(7):
+        ring.append(lax.ppermute(ring[-1], "shard", [(dev, (dev + 1) % 8) for dev in range(8)]))
+    every_image = jnp.roll(
+        jnp.concatenate(ring[::-1], axis=0),
+        (lax.axis_index("shard") + 1) * ring[0].shape[0],
+        axis=0,
+    )
 
     def fetch_pair(stored):
         picture = every_image[stored]

time: 331 us -> 300 us (0.906)
  waiting for transfers between devices: 78.4 us -> 33.4 us
  starting transfers between devices: 0.19 us -> 10.7 us
  local copies, waits for them, and re-layouts: 26.9 us -> 31.1 us
  loops' own time: 47 us -> 43.3 us
  blocking collectives: 28 us -> 31.6 us
    all_gather x1 -> x0, waiting for transfers between devices: 32.5 us -> none  [shards(): every_image = lax.all_gather(normed[None], 'shard', axis=0, tiled=True)]
    all_gather x1, waiting for transfers between devices: 24 us -> 0.01 us  [shards(): lax.all_gather(w_out, 'shard', axis=0, tiled=True)]
    all_gather x1, waiting for transfers between devices: 19.3 us -> 0.01 us  [shards(): lax.all_gather(w_value, 'shard', axis=0, tiled=True)]
    ppermute x0 -> x7, waiting for transfers between devices: none -> 16.9 us  [shards(): lax.ppermute(ring[-1], 'shard', [(dev, (dev + 1) % 8) for dev in range(8)])]
    all_gather x1, waiting for transfers between devices: 0.02 us -> 14.4 us  [shards(): lax.all_gather(w_key, 'shard', axis=0, tiled=True)]
    ppermute x0 -> x7, starting transfers between devices: none -> 10.6 us  [shards(): lax.ppermute(ring[-1], 'shard', [(dev, (dev + 1) % 8) for dev in range(8)])]
    unnamed x1, blocking collectives: 6.63 us -> 12.3 us
    all_gather x1, blocking collectives: 12 us -> 8.08 us  [shards(): lax.all_gather(pair_images, 'shard', axis=0, tiled=True)]
  transfers between devices with their start and end apart: 5 -> 11, of which waited for: 3 -> 4; matrix products, arithmetic and copies ran while one was open for 7% -> 9% of each run, Pallas kernels for 0% -> 0%
where the time goes in v1:
time: 300 us; the launch traced here: 298 us
  matrix products  116 us (39%)
  loops' own time  43.3 us (14%)
  waiting for transfers between devices  33.4 us (11%)
  blocking collectives  31.6 us (11%)
  local copies, waits for them, and re-layouts  31.1 us (10%)
  other arithmetic  18.2 us (6%)
  between operations  14.1 us (5%)
  starting transfers between devices  10.7 us (4%)
    dot_general x29, matrix products, project_rows(): jnp.dot(rows, weight, preferred_element_type=jnp.float32)  45.8 us
    another operation x1, loops' own time, shards(): lax.fori_loop(0, direction_total, one_direction, start)  43.3 us
    sub x14, matrix products, attend_many(): scores = scores - jnp.max(scores, axis=-1, keepdims=True)  33.3 us
    dot_general x14, matrix products, attend_many(): jnp.einsum('bhqk,bkhd->bqhd', attention, value_heads, preferred_element_t...  29.7 us
    ppermute x7, waiting for transfers between devices, shards(): lax.ppermute(ring[-1], 'shard', [(dev, (dev + 1) % 8) for dev in range(8)])  16.9 us
    all_gather x1, waiting for transfers between devices, shards(): lax.all_gather(w_key, 'shard', axis=0, tiled=True)  14.4 us
    unnamed x1, blocking collectives  12.3 us
    all_gather x1, blocking collectives, shards(): lax.all_gather(confidence, 'shard', axis=0, tiled=True)  11.1 us
  transfers between devices with their start and end apart: 11, of which 4 were waited for; matrix products, arithmetic and copies ran while one was open for 9% of the time, Pallas kernels for 0%

profile of v1, /device:TPU:13, one launch (start us, length us, event | category | flops | bytes accessed | tf_op | source)
XLA Modules:
  0.0 298.4 jit_solution(1808169786943829121)
XLA Ops:
  12.3 1.9 collective-permute-start
  14.2 3.7 %collective-permute-done = bf16[1,192,768]{2,1,0:T(8,128)(2,1)S(1)} collective-permute-done((bf16[1,192,768]{2,1,0:T(8,128)(2,1)S(1)}, bf16[1,192,768]{2,1,0:T(8,128)(2,1)S(1)}, u32[]{:S(2)}, u32[]{:S(2)}) %collective-permute-start) | collective-permute-done | bytes 294944 | tf_op jit(solution)/shard_map/ppermute | solution.py:69
  17.9 2.5 collective-permute-start.1
  23.1 12.3 %all-reduce = s32[8]{0:T(128)S(1)} all-reduce(s32[8]{0:T(128)S(1)} %dynamic-update-slice), channel_id=1, replica_groups=mesh['group'=4,'shard'=8] {'shard'}, use_global_device_ids=true, to_apply=%add | all-reduce | flops 8 | bytes 64
  35.4 8.1 %all-gather = s32[8,8,2]{1,2,0:T(2,128)S(1)} all-gather(s32[1,8,2]{1,2,0:T(2,128)} %bitcast.138), channel_id=1, replica_groups=mesh['group'=4,'shard'=8] {'shard'}, dimensions={0}, use_global_device_ids=true | all-gather | bytes 576 | tf_op jit(solution)/shard_map/all_gather | solution.py:81
  43.6 11.1 %all-gather.1 = s32[8,8,2]{1,2,0:T(2,128)S(1)} all-gather(s32[1,8,2]{1,2,0:T(2,128)} %bitcast.139), channel_id=1, replica_groups=mesh['group'=4,'shard'=8] {'shard'}, dimensions={0}, use_global_device_ids=true | all-gather | bytes 576 | tf_op jit(solution)/shard_map/all_gather | solution.py:82
  55.5 5.1 %fusion.31 = pred[64]{0:T(512)(128)(4,1)S(1)} fusion(s32[]{:T(128)} %bitcast.13, s32[]{:T(128)} %bitcast.14, s32[]{:T(128)} %bitcast.15, s32[]{:T(128)} %bitcast.16, s32[]{:T(128)} %bitcast.17, s32[]{:T(128)} %bitcast.19, s32[]{:T(128)} %bitcast.18, s32[]{:T(128)} %bitcast.12), kind=kLoop, calls=%fused_computation.90 | loop fusion | flops 2048 | bytes 96 | tf_op jit(solution)/shard_map/lt | solution.py:88
  60.6 1.6 fusion.37
  62.3 5.1 %bitcast_select_fusion.1 = (s32[64]{0:T(128)S(1)}, s32[64]{0:T(128)S(1)}) fusion(s32[64,2]{0,1:T(2,128)S(1)} %reshape.279, s32[]{:T(128)} %bitcast.24, s32[]{:T(128)} %bitcast.25, s32[]{:T(128)} %bitcast.26, s32[]{:T(128)} %bitcast.27, s32[]{:T(128)} %bitcast.28, s32[]{:T(128)} %bitcast.30, s32[]{:T(128)} %bitcast.29, s32[]{:T(128)} %bitcast.23), kind=kLoop, calls=%fused_computation.64 | loop fusion | flops 2176 | bytes 1056 | tf_op jit(solution)/shard_map/gather | solution.py:89
  67.5 2.5 sort.17
  71.1 10.2 %collective-permute-done.4 = bf16[1,192,768]{2,1,0:T(8,128)(2,1)S(1)} collective-permute-done((bf16[1,192,768]{2,1,0:T(8,128)(2,1)S(1)}, bf16[1,192,768]{2,1,0:T(8,128)(2,1)S(1)}, u32[]{:S(2)}, u32[]{:S(2)}) %collective-permute-start.4) | collective-permute-done | bytes 294944 | tf_op jit(solution)/shard_map/ppermute | solution.py:69
  81.3 2.6 collective-permute-start.5
  84.6 3.0 %collective-permute-done.5 = bf16[1,192,768]{2,1,0:T(8,128)(2,1)S(1)} collective-permute-done((bf16[1,192,768]{2,1,0:T(8,128)(2,1)S(1)}, bf16[1,192,768]{2,1,0:T(8,128)(2,1)S(1)}, u32[]{:S(2)}, u32[]{:S(2)}) %collective-permute-start.5) | collective-permute-done | bytes 294944 | tf_op jit(solution)/shard_map/ppermute | solution.py:69
  87.6 2.5 collective-permute-start.6
  92.7 1.9 convolution_convert_fusion.3
  95.6 1.6 constant_dynamic-slice_fusion
  97.2 14.4 %all-gather.9.cloned.1.call-done = bf16[768,768]{1,0:T(8,128)(2,1)} async-done(((bf16[96,768]{1,0:T(8,128)(2,1)}), bf16[768,768]{1,0:T(8,128)(2,1)}) %all-gather.9.cloned.1.call-update) | async-done | bytes 1179664 | tf_op jit(solution)/shard_map/all_gather | solution.py:59
  111.6 179.5 %while.12 = (s32[]{:T(128)}, f32[192,768]{1,0:T(8,128)S(1)}, f32[]{:T(128)}, s32[]{:T(128)}, s32[128]{0:T(128)S(1)}, /*index=5*/s32[128]{0:T(128)S(1)}, bf16[8,1...) while((s32[]{:T(128)}, f32[192,768]{1,0:T(8,128)S(1)}, ...), condition=%wide.region_7.8_spmd, body=%wide.region_4.7_spmd.sunk | while | flops 795672768 | bytes 21547328 | solution.py:113
  114.6 1.8 convolution_convert_fusion.8
  116.5 2.4 fusion.68
  120.5 2.1 convolution_convert_fusion.9
  127.3 1.8 convolution_convert_fusion.8
  129.3 2.4 fusion.68
  131.7 1.4 convolution_convert_fusion.7
  133.2 2.1 convolution_convert_fusion.9
  140.1 1.8 convolution_convert_fusion.8
  142.1 2.4 fusion.68
  144.5 1.4 convolution_convert_fusion.7
  146.0 2.1 convolution_convert_fusion.9
  152.9 1.8 convolution_convert_fusion.8
  154.8 2.4 fusion.68
  157.2 1.4 convolution_convert_fusion.7
  158.8 2.1 convolution_convert_fusion.9
  165.7 1.8 convolution_convert_fusion.8
  167.6 2.4 fusion.68
  170.0 1.4 convolution_convert_fusion.7
  171.6 2.1 convolution_convert_fusion.9
  178.4 1.8 convolution_convert_fusion.8
  180.4 2.4 fusion.68
  184.3 2.1 convolution_convert_fusion.9
  191.2 1.8 convolution_convert_fusion.8
  193.2 2.4 fusion.68
  197.1 2.1 convolution_convert_fusion.9
  204.0 1.8 convolution_convert_fusion.8
  205.9 2.4 fusion.68
  209.9 2.1 convolution_convert_fusion.9
  216.8 1.8 convolution_convert_fusion.8
  218.7 2.4 fusion.68
  222.7 2.1 convolution_convert_fusion.9
  229.5 1.8 convolution_convert_fusion.8
  231.5 2.4 fusion.68
  235.4 2.1 convolution_convert_fusion.9
  242.3 1.8 convolution_convert_fusion.8
  244.3 2.4 fusion.68
  248.2 2.1 convolution_convert_fusion.9
  255.1 1.8 convolution_convert_fusion.8
  257.0 2.4 fusion.68
  261.0 2.1 convolution_convert_fusion.9
  267.9 1.8 convolution_convert_fusion.8
  269.8 2.4 fusion.68
  273.8 2.1 convolution_convert_fusion.9
  280.6 1.8 convolution_convert_fusion.8
  282.6 2.4 fusion.68
  286.5 2.1 convolution_convert_fusion.9
  (199 shorter events, 57.5 us)
Async XLA Ops:
  6.5 86.1 %all-gather.11.cloned.1.call-start = ((), (), s32[]{:S(2)}) async-start(), calls=%async_computation.2 | async-start | bytes 1327104 | tf_op jit(solution)/shard_map/all_gather | solution.py:58
  7.3 89.9 %all-gather.13.cloned.1.call-start = ((), (), s32[]{:S(2)}) async-start(), calls=%async_computation.3 | async-start | bytes 1327104 | tf_op jit(solution)/shard_map/all_gather | solution.py:61
  8.0 89.2 %all-gather.7.cloned.1.call-start = ((), (), s32[]{:S(2)}) async-start(), calls=%async_computation | async-start | bytes 1327104 | tf_op jit(solution)/shard_map/all_gather | solution.py:60
  8.7 86.2 %copy-start.2 = (bf16[1,192,768]{2,1,0:T(8,128)(2,1)S(1)}, bf16[1,192,768]{2,1,0:T(8,128)(2,1)}, u32[]{:S(2)}) copy-start(bf16[1,192,768]{2,1,0:T(8,128)(2,1)} %param.12) | copy-start | bytes 884740
  8.8 86.2 %copy-start.3 = (f32[768]{0:T(1024)S(1)}, f32[768]{0:T(1024)}, u32[]{:S(2)}) copy-start(f32[768]{0:T(1024)} %param.13) | copy-start | bytes 9220
  8.8 102.8 %all-gather.9.cloned.1.call-start = ((), (), s32[]{:S(2)}) async-start(), calls=%async_computation.1 | async-start | bytes 1327104 | tf_op jit(solution)/shard_map/all_gather | solution.py:59
  12.3 5.6 %collective-permute-start = (bf16[1,192,768]{2,1,0:T(8,128)(2,1)S(1)}, bf16[1,192,768]{2,1,0:T(8,128)(2,1)S(1)}, u32[]{:S(2)}, u32[]{:S(2)}) collective-permute-start(bf16[1,192,768]{2,1,0:T(8,128)(2,1)S(1)} %fusion.19), channel_id=1, source_target_pairs={{0,1},{1,2},{2,3},{3,4},{4,5},{5,6},{6,7},{7,0},{8,9},{9,10},{10,1... | collective-permute-start | bytes 884744 | tf_op jit(solution)/shard_map/ppermute | solution.py:69
  17.9 36.9 %collective-permute-start.1 = (bf16[1,192,768]{2,1,0:T(8,128)(2,1)S(1)}, bf16[1,192,768]{2,1,0:T(8,128)(2,1)S(1)}, u32[]{:S(2)}, u32[]{:S(2)}) collective-permute-start(bf16[1,192,768]{2,1,0:T(8,128)(2,1)S(1)} %collective-permute-done), channel_id=1, source_target_pairs={{0,1},{1,2},{2,3},{3,4},{4,5},{5,6},{6,7},{7,0},{8,9},{9,10},{10,1... | collective-permute-start | bytes 884744 | tf_op jit(solution)/shard_map/ppermute | solution.py:69
  54.8 7.5 %collective-permute-start.2 = (bf16[1,192,768]{2,1,0:T(8,128)(2,1)S(1)}, bf16[1,192,768]{2,1,0:T(8,128)(2,1)S(1)}, u32[]{:S(2)}, u32[]{:S(2)}) collective-permute-start(bf16[1,192,768]{2,1,0:T(8,128)(2,1)S(1)} %collective-permute-done.1), channel_id=1, source_target_pairs={{0,1},{1,2},{2,3},{3,4},{4,5},{5,6},{6,7},{7,0},{8,9},{9,10},{10,1... | collective-permute-start | bytes 884744 | tf_op jit(solution)/shard_map/ppermute | solution.py:69
  62.3 7.8 %collective-permute-start.3 = (bf16[1,192,768]{2,1,0:T(8,128)(2,1)S(1)}, bf16[1,192,768]{2,1,0:T(8,128)(2,1)S(1)}, u32[]{:S(2)}, u32[]{:S(2)}) collective-permute-start(bf16[1,192,768]{2,1,0:T(8,128)(2,1)S(1)} %collective-permute-done.2), channel_id=1, source_target_pairs={{0,1},{1,2},{2,3},{3,4},{4,5},{5,6},{6,7},{7,0},{8,9},{9,10},{10,1... | collective-permute-start | bytes 884744 | tf_op jit(solution)/shard_map/ppermute | solution.py:69
  70.1 11.3 %collective-permute-start.4 = (bf16[1,192,768]{2,1,0:T(8,128)(2,1)S(1)}, bf16[1,192,768]{2,1,0:T(8,128)(2,1)S(1)}, u32[]{:S(2)}, u32[]{:S(2)}) collective-permute-start(bf16[1,192,768]{2,1,0:T(8,128)(2,1)S(1)} %collective-permute-done.3), channel_id=1, source_target_pairs={{0,1},{1,2},{2,3},{3,4},{4,5},{5,6},{6,7},{7,0},{8,9},{9,10},{10,1... | collective-permute-start | bytes 884744 | tf_op jit(solution)/shard_map/ppermute | solution.py:69
  81.3 6.3 %collective-permute-start.5 = (bf16[1,192,768]{2,1,0:T(8,128)(2,1)S(1)}, bf16[1,192,768]{2,1,0:T(8,128)(2,1)S(1)}, u32[]{:S(2)}, u32[]{:S(2)}) collective-permute-start(bf16[1,192,768]{2,1,0:T(8,128)(2,1)S(1)} %collective-permute-done.4), channel_id=1, source_target_pairs={{0,1},{1,2},{2,3},{3,4},{4,5},{5,6},{6,7},{7,0},{8,9},{9,10},{10,1... | collective-permute-start | bytes 884744 | tf_op jit(solution)/shard_map/ppermute | solution.py:69
  87.6 7.1 %collective-permute-start.6 = (bf16[1,192,768]{2,1,0:T(8,128)(2,1)S(1)}, bf16[1,192,768]{2,1,0:T(8,128)(2,1)S(1)}, u32[]{:S(2)}, u32[]{:S(2)}) collective-permute-start(bf16[1,192,768]{2,1,0:T(8,128)(2,1)S(1)} %collective-permute-done.5), channel_id=1, source_target_pairs={{0,1},{1,2},{2,3},{3,4},{4,5},{5,6},{6,7},{7,0},{8,9},{9,10},{10,1... | collective-permute-start | bytes 884744 | tf_op jit(solution)/shard_map/ppermute | solution.py:69
  112.3 6.6 %copy-start.1 = (bf16[768,768]{1,0:T(8,128)(2,1)S(1)}, bf16[768,768]{1,0:T(8,128)(2,1)}, u32[]{:S(2)}) copy-start(bf16[768,768]{1,0:T(8,128)(2,1)} %get-tuple-element.257) | copy-start | bytes 3538948 | tf_op jit(solution)/shard_map/while
  120.3 3.6 %copy-start = (bf16[768,768]{1,0:T(8,128)(2,1)S(1)}, bf16[768,768]{1,0:T(8,128)(2,1)}, u32[]{:S(2)}) copy-start(bf16[768,768]{1,0:T(8,128)(2,1)} %get-tuple-element.260) | copy-start | bytes 3538948 | tf_op jit(solution)/shard_map/while
  125.0 6.6 %copy-start.1 = (bf16[768,768]{1,0:T(8,128)(2,1)S(1)}, bf16[768,768]{1,0:T(8,128)(2,1)}, u32[]{:S(2)}) copy-start(bf16[768,768]{1,0:T(8,128)(2,1)} %get-tuple-element.257) | copy-start | bytes 3538948 | tf_op jit(solution)/shard_map/while
  133.0 3.6 %copy-start = (bf16[768,768]{1,0:T(8,128)(2,1)S(1)}, bf16[768,768]{1,0:T(8,128)(2,1)}, u32[]{:S(2)}) copy-start(bf16[768,768]{1,0:T(8,128)(2,1)} %get-tuple-element.260) | copy-start | bytes 3538948 | tf_op jit(solution)/shard_map/while
  137.8 6.6 %copy-start.1 = (bf16[768,768]{1,0:T(8,128)(2,1)S(1)}, bf16[768,768]{1,0:T(8,128)(2,1)}, u32[]{:S(2)}) copy-start(bf16[768,768]{1,0:T(8,128)(2,1)} %get-tuple-element.257) | copy-start | bytes 3538948 | tf_op jit(solution)/shard_map/while
  145.8 3.6 %copy-start = (bf16[768,768]{1,0:T(8,128)(2,1)S(1)}, bf16[768,768]{1,0:T(8,128)(2,1)}, u32[]{:S(2)}) copy-start(bf16[768,768]{1,0:T(8,128)(2,1)} %get-tuple-element.260) | copy-start | bytes 3538948 | tf_op jit(solution)/shard_map/while
  150.6 6.6 %copy-start.1 = (bf16[768,768]{1,0:T(8,128)(2,1)S(1)}, bf16[768,768]{1,0:T(8,128)(2,1)}, u32[]{:S(2)}) copy-start(bf16[768,768]{1,0:T(8,128)(2,1)} %get-tuple-element.257) | copy-start | bytes 3538948 | tf_op jit(solution)/shard_map/while
  158.6 3.6 %copy-start = (bf16[768,768]{1,0:T(8,128)(2,1)S(1)}, bf16[768,768]{1,0:T(8,128)(2,1)}, u32[]{:S(2)}) copy-start(bf16[768,768]{1,0:T(8,128)(2,1)} %get-tuple-element.260) | copy-start | bytes 3538948 | tf_op jit(solution)/shard_map/while
  163.4 6.6 %copy-start.1 = (bf16[768,768]{1,0:T(8,128)(2,1)S(1)}, bf16[768,768]{1,0:T(8,128)(2,1)}, u32[]{:S(2)}) copy-start(bf16[768,768]{1,0:T(8,128)(2,1)} %get-tuple-element.257) | copy-start | bytes 3538948 | tf_op jit(solution)/shard_map/while
  171.4 3.6 %copy-start = (bf16[768,768]{1,0:T(8,128)(2,1)S(1)}, bf16[768,768]{1,0:T(8,128)(2,1)}, u32[]{:S(2)}) copy-start(bf16[768,768]{1,0:T(8,128)(2,1)} %get-tuple-element.260) | copy-start | bytes 3538948 | tf_op jit(solution)/shard_map/while
  176.1 6.6 %copy-start.1 = (bf16[768,768]{1,0:T(8,128)(2,1)S(1)}, bf16[768,768]{1,0:T(8,128)(2,1)}, u32[]{:S(2)}) copy-start(bf16[768,768]{1,0:T(8,128)(2,1)} %get-tuple-element.257) | copy-start | bytes 3538948 | tf_op jit(solution)/shard_map/while
  184.1 3.6 %copy-start = (bf16[768,768]{1,0:T(8,128)(2,1)S(1)}, bf16[768,768]{1,0:T(8,128)(2,1)}, u32[]{:S(2)}) copy-start(bf16[768,768]{1,0:T(8,128)(2,1)} %get-tuple-element.260) | copy-start | bytes 3538948 | tf_op jit(solution)/shard_map/while
  188.9 6.6 %copy-start.1 = (bf16[768,768]{1,0:T(8,128)(2,1)S(1)}, bf16[768,768]{1,0:T(8,128)(2,1)}, u32[]{:S(2)}) copy-start(bf16[768,768]{1,0:T(8,128)(2,1)} %get-tuple-element.257) | copy-start | bytes 3538948 | tf_op jit(solution)/shard_map/while
  196.9 3.6 %copy-start = (bf16[768,768]{1,0:T(8,128)(2,1)S(1)}, bf16[768,768]{1,0:T(8,128)(2,1)}, u32[]{:S(2)}) copy-start(bf16[768,768]{1,0:T(8,128)(2,1)} %get-tuple-element.260) | copy-start | bytes 3538948 | tf_op jit(solution)/shard_map/while
  201.7 6.6 %copy-start.1 = (bf16[768,768]{1,0:T(8,128)(2,1)S(1)}, bf16[768,768]{1,0:T(8,128)(2,1)}, u32[]{:S(2)}) copy-start(bf16[768,768]{1,0:T(8,128)(2,1)} %get-tuple-element.257) | copy-start | bytes 3538948 | tf_op jit(solution)/shard_map/while
  209.7 3.6 %copy-start = (bf16[768,768]{1,0:T(8,128)(2,1)S(1)}, bf16[768,768]{1,0:T(8,128)(2,1)}, u32[]{:S(2)}) copy-start(bf16[768,768]{1,0:T(8,128)(2,1)} %get-tuple-element.260) | copy-start | bytes 3538948 | tf_op jit(solution)/shard_map/while
  214.5 6.6 %copy-start.1 = (bf16[768,768]{1,0:T(8,128)(2,1)S(1)}, bf16[768,768]{1,0:T(8,128)(2,1)}, u32[]{:S(2)}) copy-start(bf16[768,768]{1,0:T(8,128)(2,1)} %get-tuple-element.257) | copy-start | bytes 3538948 | tf_op jit(solution)/shard_map/while
  222.5 3.6 %copy-start = (bf16[768,768]{1,0:T(8,128)(2,1)S(1)}, bf16[768,768]{1,0:T(8,128)(2,1)}, u32[]{:S(2)}) copy-start(bf16[768,768]{1,0:T(8,128)(2,1)} %get-tuple-element.260) | copy-start | bytes 3538948 | tf_op jit(solution)/shard_map/while
  227.2 6.6 %copy-start.1 = (bf16[768,768]{1,0:T(8,128)(2,1)S(1)}, bf16[768,768]{1,0:T(8,128)(2,1)}, u32[]{:S(2)}) copy-start(bf16[768,768]{1,0:T(8,128)(2,1)} %get-tuple-element.257) | copy-start | bytes 3538948 | tf_op jit(solution)/shard_map/while
  235.2 3.6 %copy-start = (bf16[768,768]{1,0:T(8,128)(2,1)S(1)}, bf16[768,768]{1,0:T(8,128)(2,1)}, u32[]{:S(2)}) copy-start(bf16[768,768]{1,0:T(8,128)(2,1)} %get-tuple-element.260) | copy-start | bytes 3538948 | tf_op jit(solution)/shard_map/while
  240.0 6.6 %copy-start.1 = (bf16[768,768]{1,0:T(8,128)(2,1)S(1)}, bf16[768,768]{1,0:T(8,128)(2,1)}, u32[]{:S(2)}) copy-start(bf16[768,768]{1,0:T(8,128)(2,1)} %get-tuple-element.257) | copy-start | bytes 3538948 | tf_op jit(solution)/shard_map/while
  248.0 3.6 %copy-start = (bf16[768,768]{1,0:T(8,128)(2,1)S(1)}, bf16[768,768]{1,0:T(8,128)(2,1)}, u32[]{:S(2)}) copy-start(bf16[768,768]{1,0:T(8,128)(2,1)} %get-tuple-element.260) | copy-start | bytes 3538948 | tf_op jit(solution)/shard_map/while
  252.8 6.6 %copy-start.1 = (bf16[768,768]{1,0:T(8,128)(2,1)S(1)}, bf16[768,768]{1,0:T(8,128)(2,1)}, u32[]{:S(2)}) copy-start(bf16[768,768]{1,0:T(8,128)(2,1)} %get-tuple-element.257) | copy-start | bytes 3538948 | tf_op jit(solution)/shard_map/while
  260.8 3.6 %copy-start = (bf16[768,768]{1,0:T(8,128)(2,1)S(1)}, bf16[768,768]{1,0:T(8,128)(2,1)}, u32[]{:S(2)}) copy-start(bf16[768,768]{1,0:T(8,128)(2,1)} %get-tuple-element.260) | copy-start | bytes 3538948 | tf_op jit(solution)/shard_map/while
  265.6 6.6 %copy-start.1 = (bf16[768,768]{1,0:T(8,128)(2,1)S(1)}, bf16[768,768]{1,0:T(8,128)(2,1)}, u32[]{:S(2)}) copy-start(bf16[768,768]{1,0:T(8,128)(2,1)} %get-tuple-element.257) | copy-start | bytes 3538948 | tf_op jit(solution)/shard_map/while
  273.6 3.6 %copy-start = (bf16[768,768]{1,0:T(8,128)(2,1)S(1)}, bf16[768,768]{1,0:T(8,128)(2,1)}, u32[]{:S(2)}) copy-start(bf16[768,768]{1,0:T(8,128)(2,1)} %get-tuple-element.260) | copy-start | bytes 3538948 | tf_op jit(solution)/shard_map/while
  278.3 6.6 %copy-start.1 = (bf16[768,768]{1,0:T(8,128)(2,1)S(1)}, bf16[768,768]{1,0:T(8,128)(2,1)}, u32[]{:S(2)}) copy-start(bf16[768,768]{1,0:T(8,128)(2,1)} %get-tuple-element.257) | copy-start | bytes 3538948 | tf_op jit(solution)/shard_map/while
  286.3 3.6 %copy-start = (bf16[768,768]{1,0:T(8,128)(2,1)S(1)}, bf16[768,768]{1,0:T(8,128)(2,1)}, u32[]{:S(2)}) copy-start(bf16[768,768]{1,0:T(8,128)(2,1)} %get-tuple-element.260) | copy-start | bytes 3538948 | tf_op jit(solution)/shard_map/while
Sparse Core Ops, SparseCore 0:
  9.0 26.5 all-gather.10
  37.2 22.2 all-gather.12
  61.2 24.5 all-gather.6
  87.3 24.2 all-gather.8
